TPU v7x, 32 devices: a whole 2x2x4 slice. The times are simulated.
32 devices in a mesh: gx: 16 (over z, y, core), gy: 2 (over x).
Axes of the slice: x: 2, y: 2, z: 4, core: 2. Of those that a mesh axis runs over, the one named last changes fastest.
Arguments:
- tangent: bfloat16 [256, 1024, 256], P(None, 'gx', 'gy'), may hold values from -6 to 6
- courant_x: float32 [1024, 256], P('gx', 'gy'), may hold values from -0.5 to 0.5
- courant_y: float32 [1024, 256], P('gx', 'gy'), may hold values from -0.5 to 0.5
- growth: float32 [1024, 256], P('gx', 'gy'), may hold values from -0.15 to 0.15
Outputs:
- basis: bfloat16 [256, 1024, 256], P(None, 'gx', 'gy')
- factor: float32 [256, 256], replicated
- exponents: float32 [256], replicated
All inputs are finite; a program needn't handle non-finite values.
Results may differ from a plain program's by a relative error of at most 0.001.
The roundings to bfloat16 on the way count: a program that leaves them out, or rounds other values in their place, can miss the bound.
Values may be sent and summed in bfloat16 or wider, within the bound.
No kernel may reach another device: no remote copies, remote signals or barrier semaphores. Data moves between devices by JAX's collectives and lax.ppermute only.
A program may use at most 128 MiB of HBM per device.

v0:
```python
import jax
import jax.numpy as jnp
from jax import lax
from jax.sharding import PartitionSpec as P

SUBSTEPS = 4


def extended(block, sides, width):
    for axis, dim in sides:
        count = lax.axis_size(axis)
        forward = [(i, i + 1) for i in range(count - 1)]
        forward.append((count - 1, 0))
        backward = [(target, source) for source, target in forward]
        low = lax.ppermute(
            lax.slice_in_dim(block, block.shape[dim] - width, None, axis=dim), axis, forward
        )
        high = lax.ppermute(lax.slice_in_dim(block, 0, width, axis=dim), axis, backward)
        block = jnp.concatenate([low, block, high], axis=dim)
    return block


def advance(padded, courant_x, courant_y, growth):
    centre = padded[:, 1:-1, 1:-1]
    north = padded[:, 2:, 1:-1]
    south = padded[:, :-2, 1:-1]
    east = padded[:, 1:-1, 2:]
    west = padded[:, 1:-1, :-2]
    return (
        centre
        + 0.2 * (north + south + east + west - 4.0 * centre)
        - courant_x * (north - south)
        - courant_y * (east - west)
        + growth * centre
    )


def inner_products(left, right):
    return lax.dot_general(
        left, right, (((1,), (1,)), ((), ())), preferred_element_type=jnp.float32
    )


def per_device(tangent, courant_x, courant_y, growth):
    fields, rows, cols = tangent.shape
    steps = SUBSTEPS
    state = tangent.astype(jnp.float32)
    for step in range(steps):
        padded = extended(state, (("gx", 1), ("gy", 2)), 1)
        state = advance(padded, courant_x, courant_y, growth)
    evolved = state.astype(jnp.bfloat16).reshape(fields, rows * cols)
    total = jnp.float32(rows * lax.axis_size("gx") * cols * lax.axis_size("gy"))
    gram = lax.psum(inner_products(evolved, evolved), ("gx", "gy"))
    gram = gram / total
    lower = jnp.linalg.cholesky(gram)
    inverse = lax.linalg.triangular_solve(
        lower, jnp.eye(fields, dtype=jnp.float32), left_side=True, lower=True
    ).astype(jnp.bfloat16)
    basis = jnp.dot(inverse, evolved, preferred_element_type=jnp.float32)
    exponents = jnp.log(jnp.diagonal(lower))
    return (basis.astype(jnp.bfloat16).reshape(fields, rows, cols), lower.T, exponents)


def solution(mesh):
    placed = (P(None, "gx", "gy"), P("gx", "gy"), P("gx", "gy"), P("gx", "gy"))
    return jax.shard_map(
        per_device,
        mesh=mesh,
        in_specs=placed,
        out_specs=(P(None, "gx", "gy"), P(), P()),
        check_vma=False,
    )
```

profile of v0, /device:TPU:0, one launch (start us, length us, event | category | flops | bytes accessed | tf_op | source)
XLA Modules:
  0.0 358.3 jit_solution(11706130082598331027)
XLA Ops:
  7.2 6.8 %copy.53 = bf16[256,64,128]{0,2,1:T(8,128)(2,1)} copy(bf16[256,64,128]{2,1,0:T(8,128)(2,1)} %param.4) | data formatting | bytes 8388608 | tf_op args[0]
  14.0 0.9 fusion.17
  15.0 5.5 %collective-permute-start = (f32[256,1,128]{2,0,1:T(8,128)S(1)}, f32[256,1,128]{2,0,1:T(8,128)S(1)}, u32[]{:S(2)}, u32[]{:S(2)}) collective-permute-start(f32[256,1,128]{2,0,1:T(8,128)S(1)} %copy.54), channel_id=1, source_target_pairs={{2,0},{4,2},{6,4},{8,6},{10,8},{12,10},{14,12},{16,14},{18,16},{20... | collective-permute-start | bytes 393224 | tf_op jit(solution)/shard_map/ppermute | solution.py:18
  20.7 6.6 %convert_element_type.11 = f32[256,64,128]{0,2,1:T(8,128)} convert(bf16[256,64,128]{0,2,1:T(8,128)(2,1)} %copy.53) | non-fusion elementwise | flops 2097152 | bytes 12582912 | tf_op jit(solution)/shard_map/convert_element_type | solution.py:47
  27.4 0.4 collective-permute-done.1
  27.9 1.5 pad_maximum_fusion.43
  29.4 1.6 collective-permute-start.2
  30.9 0.5 collective-permute-start.3
  31.5 2.3 collective-permute-done.2
  33.9 1.4 collective-permute-done.3
  35.4 14.9 %multiply_add_fusion.2 = f32[256,64,128]{0,2,1:T(8,128)S(1)} fusion(f32[256,64,128]{0,2,1:T(8,128)S(1)} %copy-done.6, f32[256,1,128]{0,2,1:T(8,128)S(1)} %copy.55, f32[256,1,128]{0,2,1:T(8,128)S(1)} %copy.57, f32[256,66,1]{0,2,1:T(1,128)S(1)} %copy.63, f32[256,66,1]{0,2,1:T(1,128)S(1)} %copy.61, f32[64,128]{1,0:T(8,128)S(1)} %copy-done.8, ...), kind=kLoop, calls=%fused_computation.39 | loop fusion | flops 48234496 | bytes 17272832 | tf_op jit(solution)/shard_map/add | solution.py:30
  50.4 3.3 copy-done.2
  53.7 2.7 collective-permute-start.4
  56.6 2.4 collective-permute-done.4
  59.1 4.6 %collective-permute-done.5 = f32[256,1,128]{2,0,1:T(8,128)S(1)} collective-permute-done((f32[256,1,128]{2,0,1:T(8,128)S(1)}, f32[256,1,128]{2,0,1:T(8,128)S(1)}, u32[]{:S(2)}, u32[]{:S(2)}) %collective-permute-start.5) | collective-permute-done | bytes 131104 | tf_op jit(solution)/shard_map/ppermute | solution.py:15
  63.8 1.5 pad_maximum_fusion.40
  65.2 1.1 collective-permute-start.6
  66.4 1.0 collective-permute-start.7
  67.3 2.3 collective-permute-done.6
  69.7 1.0 collective-permute-done.7
  70.8 14.9 %multiply_add_fusion.1 = f32[256,64,128]{0,2,1:T(8,128)S(1)} fusion(f32[256,64,128]{0,2,1:T(8,128)S(1)} %copy-done.3, f32[256,1,128]{0,2,1:T(8,128)S(1)} %copy.65, f32[256,1,128]{0,2,1:T(8,128)S(1)} %copy.67, f32[256,66,1]{0,2,1:T(1,128)S(1)} %copy.73, f32[256,66,1]{0,2,1:T(1,128)S(1)} %copy.71, f32[64,128]{1,0:T(8,128)S(1)} %copy-done.8, ...), kind=kLoop, calls=%fused_computation.38 | loop fusion | flops 48234496 | bytes 17272832 | tf_op jit(solution)/shard_map/add | solution.py:30
  85.8 3.3 copy-done.4
  89.3 0.5 collective-permute-start.9
  89.9 1.9 collective-permute-done.8
  91.8 4.6 %collective-permute-done.9 = f32[256,1,128]{2,0,1:T(8,128)S(1)} collective-permute-done((f32[256,1,128]{2,0,1:T(8,128)S(1)}, f32[256,1,128]{2,0,1:T(8,128)S(1)}, u32[]{:S(2)}, u32[]{:S(2)}) %collective-permute-start.9) | collective-permute-done | bytes 131104 | tf_op jit(solution)/shard_map/ppermute | solution.py:15
  96.6 1.5 pad_maximum_fusion.37
  98.0 1.0 collective-permute-start.10
  99.1 1.1 collective-permute-start.11
  100.1 2.3 collective-permute-done.10
  102.5 0.9 collective-permute-done.11
  103.5 14.9 %multiply_add_fusion = f32[256,64,128]{0,2,1:T(8,128)S(1)} fusion(f32[256,64,128]{0,2,1:T(8,128)S(1)} %copy-done.5, f32[256,1,128]{0,2,1:T(8,128)S(1)} %copy.75, f32[256,1,128]{0,2,1:T(8,128)S(1)} %copy.77, f32[256,66,1]{0,2,1:T(1,128)S(1)} %copy.83, f32[256,66,1]{0,2,1:T(1,128)S(1)} %copy.81, f32[64,128]{1,0:T(8,128)S(1)} %copy-done.8, ...), kind=kLoop, calls=%fused_computation.37 | loop fusion | flops 48234496 | bytes 17272832 | tf_op jit(solution)/shard_map/add | solution.py:30
  118.4 3.3 copy-done
  122.0 0.5 collective-permute-start.13
  122.5 1.9 collective-permute-done.12
  124.5 4.6 %collective-permute-done.13 = f32[256,1,128]{2,0,1:T(8,128)S(1)} collective-permute-done((f32[256,1,128]{2,0,1:T(8,128)S(1)}, f32[256,1,128]{2,0,1:T(8,128)S(1)}, u32[]{:S(2)}, u32[]{:S(2)}) %collective-permute-start.13) | collective-permute-done | bytes 131104 | tf_op jit(solution)/shard_map/ppermute | solution.py:15
  129.2 1.5 pad_maximum_fusion.34
  130.7 1.1 collective-permute-start.14
  131.8 1.0 collective-permute-start.15
  132.8 2.3 collective-permute-done.14
  135.2 1.0 collective-permute-done.15
  136.3 15.4 %add_convert_fusion = bf16[256,64,128]{0,2,1:T(8,128)(2,1)S(1)} fusion(f32[256,64,128]{0,2,1:T(8,128)S(1)} %copy-done.1, f32[256,1,128]{0,2,1:T(8,128)S(1)} %copy.85, f32[256,1,128]{0,2,1:T(8,128)S(1)} %copy.87, f32[256,66,1]{0,2,1:T(1,128)S(1)} %copy.93, f32[256,66,1]{0,2,1:T(1,128)S(1)} %copy.91, f32[64,128]{1,0:T(8,128)S(1)} %copy-done.8, ...), kind=kLoop, calls=%fused_computation.36 | loop fusion | flops 50331648 | bytes 13078528 | tf_op jit(solution)/shard_map/convert_element_type | solution.py:51
  151.7 2.0 copy-done.7
  153.7 2.5 convolution_bitcast_fusion
  156.3 121.8 %all-reduce.3.cloned.1.call-done = f32[256,256]{0,1:T(8,128)} async-done(((f32[256,256]{0,1:T(8,128)}), f32[256,256]{0,1:T(8,128)}) %all-reduce.3.cloned.1.call-update) | async-done | bytes 262160 | tf_op jit(solution)/shard_map/psum | solution.py:53
  278.0 1.0 broadcast_multiply_fusion
  279.1 1.0 fusion.1
  280.1 11.7 %cholesky.50 = f32[128,128]{1,0:T(8,128)S(1)} custom-call(f32[128,128]{1,0:T(8,128)S(1)} %cholesky.118), custom_call_target="Cholesky" | custom-call | tf_op jit(solution)/shard_map/jit(cholesky)/cholesky | solution.py:55
  291.9 9.8 %custom-call.14 = f32[1,128,128]{1,2,0:T(8,128)S(1)} custom-call(f32[1,128,128]{2,1,0:T(8,128)S(1)} %get-tuple-element.54), custom_call_target="InvertDiagBlocksLowerTriangular" | custom-call | tf_op jit(solution)/shard_map/jit(cholesky)/cholesky | solution.py:55
  301.9 0.3 convolution_subtract_fusion.1
  302.2 11.7 %cholesky.105 = f32[128,128]{1,0:T(8,128)S(1)} custom-call(f32[128,128]{1,0:T(8,128)S(1)} %convolution_subtract_fusion.1), custom_call_target="Cholesky" | custom-call | tf_op jit(solution)/shard_map/jit(cholesky)/cholesky | solution.py:55
  314.0 0.7 compare_reduce_fusion
  316.2 4.3 %while.1 = (s32[]{:T(128)}, f32[256,256]{1,0:T(8,128)S(1)}, s32[2,2]{1,0:T(2,128)S(1)}, f32[2,128,128]{2,1,0:T(8,128)S(1)}, s32[]{:T(128)}) while((s32[]{:T(128)}, f32[256,256]{1,0:T(8,128)S(1)}, s32[2,2]{1,0:T(2,128)S(1)}, f32[2,128,128]{2,1,0:T(8,128)S(1)}, s32[]{:T(128)}) %tuple.41), condition=%wide.while_cond, body=%wide.while_body.sunk | while | flops 2 | bytes 131181 | solution.py:56
  316.3 0.6 fusion.27
  316.9 1.4 bitcast_dynamic-update-slice_fusion.2
  318.4 0.6 fusion.27
  319.0 1.4 bitcast_dynamic-update-slice_fusion.2
  320.4 19.7 %custom-call.15 = f32[2,128,128]{1,2,0:T(8,128)S(1)} custom-call(f32[2,128,128]{2,1,0:T(8,128)S(1)} %get-tuple-element.10), custom_call_target="InvertDiagBlocksLowerTriangular" | custom-call | tf_op jit(solution)/shard_map/triangular_solve | solution.py:56
  340.1 0.3 fusion.18
  340.7 0.3 convolution_convert_fusion.1
  341.0 3.5 fusion
  344.5 3.2 copy.103
  347.7 0.8 copy.98
  348.5 2.3 gather_fusion
  350.9 0.6 log.3
  (75 shorter events, 3.3 us)
Async XLA Ops:
  7.2 270.9 %all-reduce.3.cloned.1.call-start = ((), (), s32[]{:S(2)}) async-start(), calls=%async_computation | async-start | bytes 524288 | tf_op jit(solution)/shard_map/psum | solution.py:53
  15.0 12.3 %collective-permute-start = (f32[256,1,128]{2,0,1:T(8,128)S(1)}, f32[256,1,128]{2,0,1:T(8,128)S(1)}, u32[]{:S(2)}, u32[]{:S(2)}) collective-permute-start(f32[256,1,128]{2,0,1:T(8,128)S(1)} %copy.54), channel_id=1, source_target_pairs={{2,0},{4,2},{6,4},{8,6},{10,8},{12,10},{14,12},{16,14},{18,16},{20... | collective-permute-start | bytes 393224 | tf_op jit(solution)/shard_map/ppermute | solution.py:18
  20.6 14.8 %copy-start.8 = (f32[64,128]{1,0:T(8,128)S(1)}, f32[64,128]{1,0:T(8,128)}, u32[]{:S(2)}) copy-start(f32[64,128]{1,0:T(8,128)} %param.7) | copy-start | bytes 98308
  20.6 14.8 %copy-start.9 = (f32[64,128]{1,0:T(8,128)S(1)}, f32[64,128]{1,0:T(8,128)}, u32[]{:S(2)}) copy-start(f32[64,128]{1,0:T(8,128)} %param.6) | copy-start | bytes 98308
  20.7 14.7 %copy-start.10 = (f32[64,128]{1,0:T(8,128)S(1)}, f32[64,128]{1,0:T(8,128)}, u32[]{:S(2)}) copy-start(f32[64,128]{1,0:T(8,128)} %param.5) | copy-start | bytes 98308
  20.7 7.1 %collective-permute-start.1 = (f32[256,1,128]{2,0,1:T(8,128)S(1)}, f32[256,1,128]{2,0,1:T(8,128)S(1)}, u32[]{:S(2)}, u32[]{:S(2)}) collective-permute-start(f32[256,1,128]{2,0,1:T(8,128)S(1)} %copy.56), channel_id=1, source_target_pairs={{0,2},{2,4},{4,6},{6,8},{8,10},{10,12},{12,14},{14,16},{16,18},{18... | collective-permute-start | bytes 393224 | tf_op jit(solution)/shard_map/ppermute | solution.py:15
  27.9 7.5 %copy-start.6 = (f32[256,64,128]{0,2,1:T(8,128)S(1)}, f32[256,64,128]{0,2,1:T(8,128)}, u32[]{:S(2)}) copy-start(f32[256,64,128]{0,2,1:T(8,128)} %convert_element_type.11) | copy-start | bytes 25165828
  29.4 4.4 %collective-permute-start.2 = (f32[256,66,1]{0,1,2:T(8,128)S(1)}, f32[256,66,1]{0,1,2:T(8,128)S(1)}, u32[]{:S(2)}, u32[]{:S(2)}) collective-permute-start(f32[256,66,1]{0,1,2:T(8,128)S(1)} %copy.60), channel_id=1, source_target_pairs={{1,0},{0,1},{3,2},{2,3},{5,4},{4,5},{7,6},{6,7},{9,8},{8,9},{11,10... | collective-permute-start | bytes 202760 | tf_op jit(solution)/shard_map/ppermute | solution.py:18
  30.9 4.4 %collective-permute-start.3 = (f32[256,66,1]{0,1,2:T(8,128)S(1)}, f32[256,66,1]{0,1,2:T(8,128)S(1)}, u32[]{:S(2)}, u32[]{:S(2)}) collective-permute-start(f32[256,66,1]{0,1,2:T(8,128)S(1)} %copy.62), channel_id=1, source_target_pairs={{0,1},{1,0},{2,3},{3,2},{4,5},{5,4},{6,7},{7,6},{8,9},{9,8},{10,11... | collective-permute-start | bytes 202760 | tf_op jit(solution)/shard_map/ppermute | solution.py:15
  50.4 3.3 copy-start.2
  53.7 5.2 %collective-permute-start.4 = (f32[256,1,128]{2,0,1:T(8,128)S(1)}, f32[256,1,128]{2,0,1:T(8,128)S(1)}, u32[]{:S(2)}, u32[]{:S(2)}) collective-permute-start(f32[256,1,128]{2,0,1:T(8,128)S(1)} %copy.64), channel_id=1, source_target_pairs={{2,0},{4,2},{6,4},{8,6},{10,8},{12,10},{14,12},{16,14},{18,16},{20... | collective-permute-start | bytes 393224 | tf_op jit(solution)/shard_map/ppermute | solution.py:18
  56.5 7.1 %collective-permute-start.5 = (f32[256,1,128]{2,0,1:T(8,128)S(1)}, f32[256,1,128]{2,0,1:T(8,128)S(1)}, u32[]{:S(2)}, u32[]{:S(2)}) collective-permute-start(f32[256,1,128]{2,0,1:T(8,128)S(1)} %copy.66), channel_id=1, source_target_pairs={{0,2},{2,4},{4,6},{6,8},{8,10},{10,12},{12,14},{14,16},{16,18},{18... | collective-permute-start | bytes 393224 | tf_op jit(solution)/shard_map/ppermute | solution.py:15
  63.8 7.0 %copy-start.3 = (f32[256,64,128]{0,2,1:T(8,128)S(1)}, f32[256,64,128]{0,2,1:T(8,128)}, u32[]{:S(2)}) copy-start(f32[256,64,128]{0,2,1:T(8,128)} %copy-done.2) | copy-start | bytes 25165828
  65.2 4.4 %collective-permute-start.6 = (f32[256,66,1]{0,1,2:T(8,128)S(1)}, f32[256,66,1]{0,1,2:T(8,128)S(1)}, u32[]{:S(2)}, u32[]{:S(2)}) collective-permute-start(f32[256,66,1]{0,1,2:T(8,128)S(1)} %copy.70), channel_id=1, source_target_pairs={{1,0},{0,1},{3,2},{2,3},{5,4},{4,5},{7,6},{6,7},{9,8},{8,9},{11,10... | collective-permute-start | bytes 202760 | tf_op jit(solution)/shard_map/ppermute | solution.py:18
  66.4 4.4 %collective-permute-start.7 = (f32[256,66,1]{0,1,2:T(8,128)S(1)}, f32[256,66,1]{0,1,2:T(8,128)S(1)}, u32[]{:S(2)}, u32[]{:S(2)}) collective-permute-start(f32[256,66,1]{0,1,2:T(8,128)S(1)} %copy.72), channel_id=1, source_target_pairs={{0,1},{1,0},{2,3},{3,2},{4,5},{5,4},{6,7},{7,6},{8,9},{9,8},{10,11... | collective-permute-start | bytes 202760 | tf_op jit(solution)/shard_map/ppermute | solution.py:15
  85.8 3.3 copy-start.4
  89.1 2.6 collective-permute-start.8
  89.3 7.1 %collective-permute-start.9 = (f32[256,1,128]{2,0,1:T(8,128)S(1)}, f32[256,1,128]{2,0,1:T(8,128)S(1)}, u32[]{:S(2)}, u32[]{:S(2)}) collective-permute-start(f32[256,1,128]{2,0,1:T(8,128)S(1)} %copy.76), channel_id=1, source_target_pairs={{0,2},{2,4},{4,6},{6,8},{8,10},{10,12},{12,14},{14,16},{16,18},{18... | collective-permute-start | bytes 393224 | tf_op jit(solution)/shard_map/ppermute | solution.py:15
  96.5 6.9 %copy-start.5 = (f32[256,64,128]{0,2,1:T(8,128)S(1)}, f32[256,64,128]{0,2,1:T(8,128)}, u32[]{:S(2)}) copy-start(f32[256,64,128]{0,2,1:T(8,128)} %copy-done.4) | copy-start | bytes 25165828
  98.0 4.4 %collective-permute-start.10 = (f32[256,66,1]{0,1,2:T(8,128)S(1)}, f32[256,66,1]{0,1,2:T(8,128)S(1)}, u32[]{:S(2)}, u32[]{:S(2)}) collective-permute-start(f32[256,66,1]{0,1,2:T(8,128)S(1)} %copy.80), channel_id=1, source_target_pairs={{1,0},{0,1},{3,2},{2,3},{5,4},{4,5},{7,6},{6,7},{9,8},{8,9},{11,10... | collective-permute-start | bytes 202760 | tf_op jit(solution)/shard_map/ppermute | solution.py:18
  99.1 4.4 %collective-permute-start.11 = (f32[256,66,1]{0,1,2:T(8,128)S(1)}, f32[256,66,1]{0,1,2:T(8,128)S(1)}, u32[]{:S(2)}, u32[]{:S(2)}) collective-permute-start(f32[256,66,1]{0,1,2:T(8,128)S(1)} %copy.82), channel_id=1, source_target_pairs={{0,1},{1,0},{2,3},{3,2},{4,5},{5,4},{6,7},{7,6},{8,9},{9,8},{10,11... | collective-permute-start | bytes 202760 | tf_op jit(solution)/shard_map/ppermute | solution.py:15
  118.4 3.3 copy-start
  121.8 2.6 collective-permute-start.12
  122.0 7.1 %collective-permute-start.13 = (f32[256,1,128]{2,0,1:T(8,128)S(1)}, f32[256,1,128]{2,0,1:T(8,128)S(1)}, u32[]{:S(2)}, u32[]{:S(2)}) collective-permute-start(f32[256,1,128]{2,0,1:T(8,128)S(1)} %copy.86), channel_id=1, source_target_pairs={{0,2},{2,4},{4,6},{6,8},{8,10},{10,12},{12,14},{14,16},{16,18},{18... | collective-permute-start | bytes 393224 | tf_op jit(solution)/shard_map/ppermute | solution.py:15
  129.2 7.0 %copy-start.1 = (f32[256,64,128]{0,2,1:T(8,128)S(1)}, f32[256,64,128]{0,2,1:T(8,128)}, u32[]{:S(2)}) copy-start(f32[256,64,128]{0,2,1:T(8,128)} %copy-done) | copy-start | bytes 25165828
  130.7 4.4 %collective-permute-start.14 = (f32[256,66,1]{0,1,2:T(8,128)S(1)}, f32[256,66,1]{0,1,2:T(8,128)S(1)}, u32[]{:S(2)}, u32[]{:S(2)}) collective-permute-start(f32[256,66,1]{0,1,2:T(8,128)S(1)} %copy.90), channel_id=1, source_target_pairs={{1,0},{0,1},{3,2},{2,3},{5,4},{4,5},{7,6},{6,7},{9,8},{8,9},{11,10... | collective-permute-start | bytes 202760 | tf_op jit(solution)/shard_map/ppermute | solution.py:18
  131.8 4.4 %collective-permute-start.15 = (f32[256,66,1]{0,1,2:T(8,128)S(1)}, f32[256,66,1]{0,1,2:T(8,128)S(1)}, u32[]{:S(2)}, u32[]{:S(2)}) collective-permute-start(f32[256,66,1]{0,1,2:T(8,128)S(1)} %copy.92), channel_id=1, source_target_pairs={{0,1},{1,0},{2,3},{3,2},{4,5},{5,4},{6,7},{7,6},{8,9},{9,8},{10,11... | collective-permute-start | bytes 202760 | tf_op jit(solution)/shard_map/ppermute | solution.py:15
  151.7 2.0 copy-start.7
Sparse Core Ops, SparseCore 0:
  156.3 121.6 all-reduce.2
where the time goes:
time: 359 us; the launch traced here: 358 us
  waiting for transfers between devices  156 us (43%)
  other arithmetic  128 us (36%)
  local copies, waits for them, and re-layouts  32.9 us (9%)
  starting transfers between devices  17.9 us (5%)
  between operations  15.9 us (4%)
  matrix products  7.3 us (2%)
    psum x1, waiting for transfers between devices, per_device(): gram = lax.psum(inner_products(evolved, evolved), ('gx', 'gy'))  122 us
    add x3, other arithmetic, advance(): centre + 0.2 * (north + south + east + west - 4.0 * centre)  44.8 us
    another operation x6, other arithmetic, per_device(): lower = jnp.linalg.cholesky(gram)  34 us
    unnamed x25, local copies, waits for them, and re-layouts  22.7 us
    another operation x3, other arithmetic, per_device(): lax.linalg.triangular_solve(lower, jnp.eye(fields, dtype=jnp.float32), le...  19.7 us
    ppermute x8, waiting for transfers between devices, extended(): lax.ppermute(lax.slice_in_dim(block, block.shape[dim] - width, None, axis...  18.5 us
    convert_element_type x1, other arithmetic, per_device(): evolved = state.astype(jnp.bfloat16).reshape(fields, rows * cols)  15.4 us
    ppermute x8, waiting for transfers between devices, extended(): lax.ppermute(lax.slice_in_dim(block, 0, width, axis=dim), axis, backward)  15.4 us
  transfers between devices with their start and end apart: 17, of which 16 were waited for; matrix products, arithmetic and copies ran while one was open for 2% of the time, Pallas kernels for 0%

commit v1 on v0

--- a/solution.py
+++ b/solution.py
@@ -2,6 +2,7 @@
 import jax.numpy as jnp
 from jax import lax
 from jax.sharding import PartitionSpec as P
+from jax.lax import all_gather
 
 SUBSTEPS = 4
 
@@ -50,7 +51,8 @@
         state = advance(padded, courant_x, courant_y, growth)
     evolved = state.astype(jnp.bfloat16).reshape(fields, rows * cols)
     total = jnp.float32(rows * lax.axis_size("gx") * cols * lax.axis_size("gy"))
-    gram = lax.psum(inner_products(evolved, evolved), ("gx", "gy"))
+    raise_marks = lambda vec, mesh_ax: jnp.sum(all_gather(vec, mesh_ax), axis=0)
+    gram = raise_marks(inner_products(evolved, evolved), ("gx", "gy"))
     gram = gram / total
     lower = jnp.linalg.cholesky(gram)
     inverse = lax.linalg.triangular_solve(

time: 359 us -> 313 us (0.87)
  waiting for transfers between devices: 156 us -> 108 us
    psum x1 -> x0, waiting for transfers between devices: 122 us -> none  [per_device(): gram = lax.psum(inner_products(evolved, evolved), ('gx', 'gy'))]
    all_gather x0 -> x1, waiting for transfers between devices: none -> 74.1 us  [per_device(): raise_marks = lambda vec, mesh_ax: jnp.sum(all_gather(vec, mesh_ax), axis=0)]
    reduce_sum x0 -> x1, other arithmetic: none -> 3.94 us  [per_device(): raise_marks = lambda vec, mesh_ax: jnp.sum(all_gather(vec, mesh_ax), axis=0)]
where the time goes in v1:
time: 313 us; the launch traced here: 312 us
  other arithmetic  130 us (42%)
  waiting for transfers between devices  108 us (35%)
  local copies, waits for them, and re-layouts  32.9 us (11%)
  starting transfers between devices  17.9 us (6%)
  between operations  16.2 us (5%)
  matrix products  6.77 us (2%)
    all_gather x1, waiting for transfers between devices, per_device(): raise_marks = lambda vec, mesh_ax: jnp.sum(all_gather(vec, mesh_ax), axis=0)  74.1 us
    add x3, other arithmetic, advance(): centre + 0.2 * (north + south + east + west - 4.0 * centre)  44.8 us
    another operation x6, other arithmetic, per_device(): lower = jnp.linalg.cholesky(gram)  34 us
    unnamed x25, local copies, waits for them, and re-layouts  22.7 us
    another operation x3, other arithmetic, per_device(): lax.linalg.triangular_solve(lower, jnp.eye(fields, dtype=jnp.float32), le...  19.7 us
    ppermute x8, waiting for transfers between devices, extended(): lax.ppermute(lax.slice_in_dim(block, block.shape[dim] - width, None, axis...  18.5 us
    convert_element_type x1, other arithmetic, per_device(): evolved = state.astype(jnp.bfloat16).reshape(fields, rows * cols)  15.4 us
    ppermute x8, waiting for transfers between devices, extended(): lax.ppermute(lax.slice_in_dim(block, 0, width, axis=dim), axis, backward)  15.4 us
  transfers between devices with their start and end apart: 17, of which 16 were waited for; matrix products, arithmetic and copies ran while one was open for 2% of the time, Pallas kernels for 0%

profile of v1, /device:TPU:0, one launch (start us, length us, event | category | flops | bytes accessed | tf_op | source)
XLA Modules:
  0.0 312.2 jit_solution(4033694122461179209)
XLA Ops:
  7.2 6.8 %copy.50 = bf16[256,64,128]{0,2,1:T(8,128)(2,1)} copy(bf16[256,64,128]{2,1,0:T(8,128)(2,1)} %param.4) | data formatting | bytes 8388608 | tf_op args[0]
  14.0 0.9 fusion.17
  15.0 5.5 %collective-permute-start = (f32[256,1,128]{2,0,1:T(8,128)S(1)}, f32[256,1,128]{2,0,1:T(8,128)S(1)}, u32[]{:S(2)}, u32[]{:S(2)}) collective-permute-start(f32[256,1,128]{2,0,1:T(8,128)S(1)} %copy.51), channel_id=1, source_target_pairs={{2,0},{4,2},{6,4},{8,6},{10,8},{12,10},{14,12},{16,14},{18,16},{20... | collective-permute-start | bytes 393224 | tf_op jit(solution)/shard_map/ppermute | solution.py:19
  20.7 6.6 %convert_element_type.11 = f32[256,64,128]{0,2,1:T(8,128)} convert(bf16[256,64,128]{0,2,1:T(8,128)(2,1)} %copy.50) | non-fusion elementwise | flops 2097152 | bytes 12582912 | tf_op jit(solution)/shard_map/convert_element_type | solution.py:48
  27.4 0.4 collective-permute-done.1
  27.9 1.5 pad_maximum_fusion.43
  29.4 1.6 collective-permute-start.2
  30.9 0.5 collective-permute-start.3
  31.5 2.3 collective-permute-done.2
  33.9 1.4 collective-permute-done.3
  35.4 14.9 %multiply_add_fusion.2 = f32[256,64,128]{0,2,1:T(8,128)S(1)} fusion(f32[256,64,128]{0,2,1:T(8,128)S(1)} %copy-done.7, f32[256,1,128]{0,2,1:T(8,128)S(1)} %copy.52, f32[256,1,128]{0,2,1:T(8,128)S(1)} %copy.54, f32[256,66,1]{0,2,1:T(1,128)S(1)} %copy.60, f32[256,66,1]{0,2,1:T(1,128)S(1)} %copy.58, f32[64,128]{1,0:T(8,128)S(1)} %copy-done.8, ...), kind=kLoop, calls=%fused_computation.39 | loop fusion | flops 48234496 | bytes 17272832 | tf_op jit(solution)/shard_map/add | solution.py:31
  50.4 3.3 %copy-done.1 = f32[256,64,128]{0,2,1:T(8,128)} copy-done((f32[256,64,128]{0,2,1:T(8,128)}, f32[256,64,128]{0,2,1:T(8,128)S(1)}, u32[]{:S(2)}) %copy-start.1) | copy-done | bytes 8388632
  53.7 2.7 collective-permute-start.4
  56.6 2.4 collective-permute-done.4
  59.1 4.6 %collective-permute-done.5 = f32[256,1,128]{2,0,1:T(8,128)S(1)} collective-permute-done((f32[256,1,128]{2,0,1:T(8,128)S(1)}, f32[256,1,128]{2,0,1:T(8,128)S(1)}, u32[]{:S(2)}, u32[]{:S(2)}) %collective-permute-start.5) | collective-permute-done | bytes 131104 | tf_op jit(solution)/shard_map/ppermute | solution.py:16
  63.8 1.5 pad_maximum_fusion.40
  65.2 1.1 collective-permute-start.6
  66.4 1.0 collective-permute-start.7
  67.3 2.3 collective-permute-done.6
  69.7 1.0 collective-permute-done.7
  70.8 14.9 %multiply_add_fusion.1 = f32[256,64,128]{0,2,1:T(8,128)S(1)} fusion(f32[256,64,128]{0,2,1:T(8,128)S(1)} %copy-done.2, f32[256,1,128]{0,2,1:T(8,128)S(1)} %copy.62, f32[256,1,128]{0,2,1:T(8,128)S(1)} %copy.64, f32[256,66,1]{0,2,1:T(1,128)S(1)} %copy.70, f32[256,66,1]{0,2,1:T(1,128)S(1)} %copy.68, f32[64,128]{1,0:T(8,128)S(1)} %copy-done.8, ...), kind=kLoop, calls=%fused_computation.38 | loop fusion | flops 48234496 | bytes 17272832 | tf_op jit(solution)/shard_map/add | solution.py:31
  85.8 3.3 %copy-done.3 = f32[256,64,128]{0,2,1:T(8,128)} copy-done((f32[256,64,128]{0,2,1:T(8,128)}, f32[256,64,128]{0,2,1:T(8,128)S(1)}, u32[]{:S(2)}) %copy-start.3) | copy-done | bytes 8388632
  89.3 0.5 collective-permute-start.9
  89.9 1.9 collective-permute-done.8
  91.8 4.6 %collective-permute-done.9 = f32[256,1,128]{2,0,1:T(8,128)S(1)} collective-permute-done((f32[256,1,128]{2,0,1:T(8,128)S(1)}, f32[256,1,128]{2,0,1:T(8,128)S(1)}, u32[]{:S(2)}, u32[]{:S(2)}) %collective-permute-start.9) | collective-permute-done | bytes 131104 | tf_op jit(solution)/shard_map/ppermute | solution.py:16
  96.6 1.5 pad_maximum_fusion.37
  98.0 1.0 collective-permute-start.10
  99.1 1.1 collective-permute-start.11
  100.1 2.3 collective-permute-done.10
  102.5 0.9 collective-permute-done.11
  103.5 14.9 %multiply_add_fusion = f32[256,64,128]{0,2,1:T(8,128)S(1)} fusion(f32[256,64,128]{0,2,1:T(8,128)S(1)} %copy-done.4, f32[256,1,128]{0,2,1:T(8,128)S(1)} %copy.72, f32[256,1,128]{0,2,1:T(8,128)S(1)} %copy.74, f32[256,66,1]{0,2,1:T(1,128)S(1)} %copy.80, f32[256,66,1]{0,2,1:T(1,128)S(1)} %copy.78, f32[64,128]{1,0:T(8,128)S(1)} %copy-done.8, ...), kind=kLoop, calls=%fused_computation.37 | loop fusion | flops 48234496 | bytes 17272832 | tf_op jit(solution)/shard_map/add | solution.py:31
  118.5 3.3 %copy-done.5 = f32[256,64,128]{0,2,1:T(8,128)} copy-done((f32[256,64,128]{0,2,1:T(8,128)}, f32[256,64,128]{0,2,1:T(8,128)S(1)}, u32[]{:S(2)}) %copy-start.5) | copy-done | bytes 8388632
  122.0 0.5 collective-permute-start.13
  122.5 1.9 collective-permute-done.12
  124.5 4.6 %collective-permute-done.13 = f32[256,1,128]{2,0,1:T(8,128)S(1)} collective-permute-done((f32[256,1,128]{2,0,1:T(8,128)S(1)}, f32[256,1,128]{2,0,1:T(8,128)S(1)}, u32[]{:S(2)}, u32[]{:S(2)}) %collective-permute-start.13) | collective-permute-done | bytes 131104 | tf_op jit(solution)/shard_map/ppermute | solution.py:16
  129.2 1.5 pad_maximum_fusion.34
  130.7 1.1 collective-permute-start.14
  131.8 1.0 collective-permute-start.15
  132.8 2.3 collective-permute-done.14
  135.2 1.0 collective-permute-done.15
  136.3 15.4 %add_convert_fusion = bf16[256,64,128]{0,2,1:T(8,128)(2,1)S(1)} fusion(f32[256,64,128]{0,2,1:T(8,128)S(1)} %copy-done.6, f32[256,1,128]{0,2,1:T(8,128)S(1)} %copy.82, f32[256,1,128]{0,2,1:T(8,128)S(1)} %copy.84, f32[256,66,1]{0,2,1:T(1,128)S(1)} %copy.90, f32[256,66,1]{0,2,1:T(1,128)S(1)} %copy.88, f32[64,128]{1,0:T(8,128)S(1)} %copy-done.8, ...), kind=kLoop, calls=%fused_computation.36 | loop fusion | flops 50331648 | bytes 13078528 | tf_op jit(solution)/shard_map/convert_element_type | solution.py:52
  151.7 2.0 copy-done
  153.7 2.0 convolution_bitcast_fusion
  155.8 74.1 %all-gather.3.cloned.1.call-done = f32[8192,256]{1,0:T(8,128)} async-done(((f32[256,256]{1,0:T(8,128)}), f32[8192,256]{1,0:T(8,128)}) %all-gather.3.cloned.1.call-update) | async-done | bytes 8388624 | tf_op jit(solution)/shard_map/all_gather | solution.py:54
  229.9 3.9 %reduce_sum.11 = f32[256,256]{1,0:T(8,128)S(1)} reduce(f32[32,256,256]{2,1,0:T(8,128)} %bitcast.48, f32[]{:T(128)} %constant.84.clone.1), dimensions={0}, to_apply=%region_0.0 | reduce | flops 2031616 | bytes 8650756 | tf_op jit(solution)/shard_map/reduce_sum | solution.py:54
  234.0 11.7 %cholesky.50 = f32[128,128]{1,0:T(8,128)S(1)} custom-call(f32[128,128]{1,0:T(8,128)S(1)} %cholesky.118), custom_call_target="Cholesky" | custom-call | tf_op jit(solution)/shard_map/jit(cholesky)/cholesky | solution.py:57
  245.8 9.8 %custom-call.14 = f32[1,128,128]{1,2,0:T(8,128)S(1)} custom-call(f32[1,128,128]{2,1,0:T(8,128)S(1)} %get-tuple-element.54), custom_call_target="InvertDiagBlocksLowerTriangular" | custom-call | tf_op jit(solution)/shard_map/jit(cholesky)/cholesky | solution.py:57
  255.8 0.3 convolution_subtract_fusion.1
  256.1 11.7 %cholesky.105 = f32[128,128]{1,0:T(8,128)S(1)} custom-call(f32[128,128]{1,0:T(8,128)S(1)} %convolution_subtract_fusion.1), custom_call_target="Cholesky" | custom-call | tf_op jit(solution)/shard_map/jit(cholesky)/cholesky | solution.py:57
  268.0 0.7 compare_reduce_fusion
  270.2 4.1 %while.1 = (s32[]{:T(128)}, f32[256,256]{1,0:T(8,128)S(1)}, s32[2,2]{1,0:T(2,128)S(1)}, f32[2,128,128]{2,1,0:T(8,128)S(1)}, s32[]{:T(128)}) while((s32[]{:T(128)}, f32[256,256]{1,0:T(8,128)S(1)}, s32[2,2]{1,0:T(2,128)S(1)}, f32[2,128,128]{2,1,0:T(8,128)S(1)}, s32[]{:T(128)}) %tuple.41), condition=%wide.while_cond, body=%wide.while_body.sunk | while | flops 2 | bytes 131181 | solution.py:58
  270.2 0.6 fusion.27
  270.8 1.4 bitcast_dynamic-update-slice_fusion.2
  272.3 0.6 fusion.27
  272.9 1.4 bitcast_dynamic-update-slice_fusion.2
  274.3 19.7 %custom-call.15 = f32[2,128,128]{1,2,0:T(8,128)S(1)} custom-call(f32[2,128,128]{2,1,0:T(8,128)S(1)} %get-tuple-element.10), custom_call_target="InvertDiagBlocksLowerTriangular" | custom-call | tf_op jit(solution)/shard_map/triangular_solve | solution.py:58
  294.0 0.3 fusion.18
  294.3 0.3 convolution_subtract_fusion
  294.5 0.3 convolution_convert_fusion.1
  294.9 3.5 %fusion = bf16[32,8,64,128]{3,1,2,0:T(8,128)(2,1)S(1)} fusion(bf16[256,8192]{0,1:T(8,128)(2,1)} %bitcast.45, bf16[128,256]{1,0:T(8,128)(2,1)S(1)} %convolution_convert_fusion.1, bf16[128,256]{1,0:T(8,128)(2,1)S(1)} %get-tuple-element.57), kind=kOutput, calls=%fused_computation.40 | convolution fusion | flops 1076101120 | bytes 8519680 | tf_op jit(solution)/shard_map/dot_general | solution.py:61
  298.3 3.2 %copy.97 = bf16[32,8,64,128]{3,2,1,0:T(8,128)(2,1)} copy(bf16[32,8,64,128]{3,1,2,0:T(8,128)(2,1)S(1)} %fusion) | data formatting | bytes 8388608
  301.6 0.8 copy.94
  302.4 2.3 gather_fusion
  304.7 0.6 log.3
  (75 shorter events, 3.1 us)
Async XLA Ops:
  7.2 222.7 %all-gather.3.cloned.1.call-start = ((), (), s32[]{:S(2)}) async-start(), calls=%async_computation | async-start | bytes 8650752 | tf_op jit(solution)/shard_map/all_gather | solution.py:54
  15.0 12.3 %collective-permute-start = (f32[256,1,128]{2,0,1:T(8,128)S(1)}, f32[256,1,128]{2,0,1:T(8,128)S(1)}, u32[]{:S(2)}, u32[]{:S(2)}) collective-permute-start(f32[256,1,128]{2,0,1:T(8,128)S(1)} %copy.51), channel_id=1, source_target_pairs={{2,0},{4,2},{6,4},{8,6},{10,8},{12,10},{14,12},{16,14},{18,16},{20... | collective-permute-start | bytes 393224 | tf_op jit(solution)/shard_map/ppermute | solution.py:19
  20.6 14.8 %copy-start.8 = (f32[64,128]{1,0:T(8,128)S(1)}, f32[64,128]{1,0:T(8,128)}, u32[]{:S(2)}) copy-start(f32[64,128]{1,0:T(8,128)} %param.7) | copy-start | bytes 98308
  20.6 14.8 %copy-start.9 = (f32[64,128]{1,0:T(8,128)S(1)}, f32[64,128]{1,0:T(8,128)}, u32[]{:S(2)}) copy-start(f32[64,128]{1,0:T(8,128)} %param.6) | copy-start | bytes 98308
  20.7 14.7 %copy-start.10 = (f32[64,128]{1,0:T(8,128)S(1)}, f32[64,128]{1,0:T(8,128)}, u32[]{:S(2)}) copy-start(f32[64,128]{1,0:T(8,128)} %param.5) | copy-start | bytes 98308
  20.7 7.1 %collective-permute-start.1 = (f32[256,1,128]{2,0,1:T(8,128)S(1)}, f32[256,1,128]{2,0,1:T(8,128)S(1)}, u32[]{:S(2)}, u32[]{:S(2)}) collective-permute-start(f32[256,1,128]{2,0,1:T(8,128)S(1)} %copy.53), channel_id=1, source_target_pairs={{0,2},{2,4},{4,6},{6,8},{8,10},{10,12},{12,14},{14,16},{16,18},{18... | collective-permute-start | bytes 393224 | tf_op jit(solution)/shard_map/ppermute | solution.py:16
  27.9 7.5 %copy-start.7 = (f32[256,64,128]{0,2,1:T(8,128)S(1)}, f32[256,64,128]{0,2,1:T(8,128)}, u32[]{:S(2)}) copy-start(f32[256,64,128]{0,2,1:T(8,128)} %convert_element_type.11) | copy-start | bytes 25165828
  29.4 4.4 %collective-permute-start.2 = (f32[256,66,1]{0,1,2:T(8,128)S(1)}, f32[256,66,1]{0,1,2:T(8,128)S(1)}, u32[]{:S(2)}, u32[]{:S(2)}) collective-permute-start(f32[256,66,1]{0,1,2:T(8,128)S(1)} %copy.57), channel_id=1, source_target_pairs={{1,0},{0,1},{3,2},{2,3},{5,4},{4,5},{7,6},{6,7},{9,8},{8,9},{11,10... | collective-permute-start | bytes 202760 | tf_op jit(solution)/shard_map/ppermute | solution.py:19
  30.9 4.4 %collective-permute-start.3 = (f32[256,66,1]{0,1,2:T(8,128)S(1)}, f32[256,66,1]{0,1,2:T(8,128)S(1)}, u32[]{:S(2)}, u32[]{:S(2)}) collective-permute-start(f32[256,66,1]{0,1,2:T(8,128)S(1)} %copy.59), channel_id=1, source_target_pairs={{0,1},{1,0},{2,3},{3,2},{4,5},{5,4},{6,7},{7,6},{8,9},{9,8},{10,11... | collective-permute-start | bytes 202760 | tf_op jit(solution)/shard_map/ppermute | solution.py:16
  50.4 3.3 %copy-start.1 = (f32[256,64,128]{0,2,1:T(8,128)}, f32[256,64,128]{0,2,1:T(8,128)S(1)}, u32[]{:S(2)}) copy-start(f32[256,64,128]{0,2,1:T(8,128)S(1)} %multiply_add_fusion.2) | copy-start | bytes 25165828
  53.7 5.2 %collective-permute-start.4 = (f32[256,1,128]{2,0,1:T(8,128)S(1)}, f32[256,1,128]{2,0,1:T(8,128)S(1)}, u32[]{:S(2)}, u32[]{:S(2)}) collective-permute-start(f32[256,1,128]{2,0,1:T(8,128)S(1)} %copy.61), channel_id=1, source_target_pairs={{2,0},{4,2},{6,4},{8,6},{10,8},{12,10},{14,12},{16,14},{18,16},{20... | collective-permute-start | bytes 393224 | tf_op jit(solution)/shard_map/ppermute | solution.py:19
  56.5 7.1 %collective-permute-start.5 = (f32[256,1,128]{2,0,1:T(8,128)S(1)}, f32[256,1,128]{2,0,1:T(8,128)S(1)}, u32[]{:S(2)}, u32[]{:S(2)}) collective-permute-start(f32[256,1,128]{2,0,1:T(8,128)S(1)} %copy.63), channel_id=1, source_target_pairs={{0,2},{2,4},{4,6},{6,8},{8,10},{10,12},{12,14},{14,16},{16,18},{18... | collective-permute-start | bytes 393224 | tf_op jit(solution)/shard_map/ppermute | solution.py:16
  63.8 7.0 %copy-start.2 = (f32[256,64,128]{0,2,1:T(8,128)S(1)}, f32[256,64,128]{0,2,1:T(8,128)}, u32[]{:S(2)}) copy-start(f32[256,64,128]{0,2,1:T(8,128)} %copy-done.1) | copy-start | bytes 25165828
  65.2 4.4 %collective-permute-start.6 = (f32[256,66,1]{0,1,2:T(8,128)S(1)}, f32[256,66,1]{0,1,2:T(8,128)S(1)}, u32[]{:S(2)}, u32[]{:S(2)}) collective-permute-start(f32[256,66,1]{0,1,2:T(8,128)S(1)} %copy.67), channel_id=1, source_target_pairs={{1,0},{0,1},{3,2},{2,3},{5,4},{4,5},{7,6},{6,7},{9,8},{8,9},{11,10... | collective-permute-start | bytes 202760 | tf_op jit(solution)/shard_map/ppermute | solution.py:19
  66.4 4.4 %collective-permute-start.7 = (f32[256,66,1]{0,1,2:T(8,128)S(1)}, f32[256,66,1]{0,1,2:T(8,128)S(1)}, u32[]{:S(2)}, u32[]{:S(2)}) collective-permute-start(f32[256,66,1]{0,1,2:T(8,128)S(1)} %copy.69), channel_id=1, source_target_pairs={{0,1},{1,0},{2,3},{3,2},{4,5},{5,4},{6,7},{7,6},{8,9},{9,8},{10,11... | collective-permute-start | bytes 202760 | tf_op jit(solution)/shard_map/ppermute | solution.py:16
  85.8 3.3 %copy-start.3 = (f32[256,64,128]{0,2,1:T(8,128)}, f32[256,64,128]{0,2,1:T(8,128)S(1)}, u32[]{:S(2)}) copy-start(f32[256,64,128]{0,2,1:T(8,128)S(1)} %multiply_add_fusion.1) | copy-start | bytes 25165828
  89.1 2.6 collective-permute-start.8
  89.3 7.1 %collective-permute-start.9 = (f32[256,1,128]{2,0,1:T(8,128)S(1)}, f32[256,1,128]{2,0,1:T(8,128)S(1)}, u32[]{:S(2)}, u32[]{:S(2)}) collective-permute-start(f32[256,1,128]{2,0,1:T(8,128)S(1)} %copy.73), channel_id=1, source_target_pairs={{0,2},{2,4},{4,6},{6,8},{8,10},{10,12},{12,14},{14,16},{16,18},{18... | collective-permute-start | bytes 393224 | tf_op jit(solution)/shard_map/ppermute | solution.py:16
  96.6 6.9 %copy-start.4 = (f32[256,64,128]{0,2,1:T(8,128)S(1)}, f32[256,64,128]{0,2,1:T(8,128)}, u32[]{:S(2)}) copy-start(f32[256,64,128]{0,2,1:T(8,128)} %copy-done.3) | copy-start | bytes 25165828
  98.0 4.4 %collective-permute-start.10 = (f32[256,66,1]{0,1,2:T(8,128)S(1)}, f32[256,66,1]{0,1,2:T(8,128)S(1)}, u32[]{:S(2)}, u32[]{:S(2)}) collective-permute-start(f32[256,66,1]{0,1,2:T(8,128)S(1)} %copy.77), channel_id=1, source_target_pairs={{1,0},{0,1},{3,2},{2,3},{5,4},{4,5},{7,6},{6,7},{9,8},{8,9},{11,10... | collective-permute-start | bytes 202760 | tf_op jit(solution)/shard_map/ppermute | solution.py:19
  99.1 4.4 %collective-permute-start.11 = (f32[256,66,1]{0,1,2:T(8,128)S(1)}, f32[256,66,1]{0,1,2:T(8,128)S(1)}, u32[]{:S(2)}, u32[]{:S(2)}) collective-permute-start(f32[256,66,1]{0,1,2:T(8,128)S(1)} %copy.79), channel_id=1, source_target_pairs={{0,1},{1,0},{2,3},{3,2},{4,5},{5,4},{6,7},{7,6},{8,9},{9,8},{10,11... | collective-permute-start | bytes 202760 | tf_op jit(solution)/shard_map/ppermute | solution.py:16
  118.4 3.3 %copy-start.5 = (f32[256,64,128]{0,2,1:T(8,128)}, f32[256,64,128]{0,2,1:T(8,128)S(1)}, u32[]{:S(2)}) copy-start(f32[256,64,128]{0,2,1:T(8,128)S(1)} %multiply_add_fusion) | copy-start | bytes 25165828
  121.8 2.6 collective-permute-start.12
  122.0 7.1 %collective-permute-start.13 = (f32[256,1,128]{2,0,1:T(8,128)S(1)}, f32[256,1,128]{2,0,1:T(8,128)S(1)}, u32[]{:S(2)}, u32[]{:S(2)}) collective-permute-start(f32[256,1,128]{2,0,1:T(8,128)S(1)} %copy.83), channel_id=1, source_target_pairs={{0,2},{2,4},{4,6},{6,8},{8,10},{10,12},{12,14},{14,16},{16,18},{18... | collective-permute-start | bytes 393224 | tf_op jit(solution)/shard_map/ppermute | solution.py:16
  129.2 7.0 %copy-start.6 = (f32[256,64,128]{0,2,1:T(8,128)S(1)}, f32[256,64,128]{0,2,1:T(8,128)}, u32[]{:S(2)}) copy-start(f32[256,64,128]{0,2,1:T(8,128)} %copy-done.5) | copy-start | bytes 25165828
  130.7 4.4 %collective-permute-start.14 = (f32[256,66,1]{0,1,2:T(8,128)S(1)}, f32[256,66,1]{0,1,2:T(8,128)S(1)}, u32[]{:S(2)}, u32[]{:S(2)}) collective-permute-start(f32[256,66,1]{0,1,2:T(8,128)S(1)} %copy.87), channel_id=1, source_target_pairs={{1,0},{0,1},{3,2},{2,3},{5,4},{4,5},{7,6},{6,7},{9,8},{8,9},{11,10... | collective-permute-start | bytes 202760 | tf_op jit(solution)/shard_map/ppermute | solution.py:19
  131.8 4.4 %collective-permute-start.15 = (f32[256,66,1]{0,1,2:T(8,128)S(1)}, f32[256,66,1]{0,1,2:T(8,128)S(1)}, u32[]{:S(2)}, u32[]{:S(2)}) collective-permute-start(f32[256,66,1]{0,1,2:T(8,128)S(1)} %copy.89), channel_id=1, source_target_pairs={{0,1},{1,0},{2,3},{3,2},{4,5},{5,4},{6,7},{7,6},{8,9},{9,8},{10,11... | collective-permute-start | bytes 202760 | tf_op jit(solution)/shard_map/ppermute | solution.py:16
  151.7 2.0 copy-start
Sparse Core Ops, SparseCore 0:
  155.8 73.9 all-gather.2
